TPU v7x, 256 devices: a whole 4x4x8 slice. The times are simulated.
256 devices in a mesh: rows: 32 (over x, y, core), grp: 8 (over z).
Axes of the slice: x: 4, y: 4, z: 8, core: 2. Of those that a mesh axis runs over, the one named last changes fastest.
Arguments:
- residual_in: float32 [65536, 128], P(('rows', 'grp')), may hold values from -6 to 6
- solution_in: float32 [65536, 128], P(('rows', 'grp')), may hold values from -6 to 6
- descriptors: float32 [32, 65536], P(None, ('rows', 'grp')), may hold values from -6 to 6
- length_weights: float32 [32], replicated, may hold values from 0.015625 to 0.125
- amplitude: float32 [1], replicated, may hold values from 0.05 to 0.15
- noise: float32 [1], replicated, may hold values from 0.5 to 1.5
- block_inverse: float32 [2, 1024, 1024], P(None, 'grp'), may hold values from -2 to 2, as said below
- block_rows: int32 [2, 1024], replicated, may hold values from 0 to 65535, as said below
Outputs:
- solution_field: float32 [65536, 128], P(('rows', 'grp'))
- residual_field: float32 [65536, 128], P(('rows', 'grp'))
Inputs may be any that keep to these rules, and one draw needn't show every extreme that they name: `block_rows`: for each step the 1024 rows are distinct; at most 16 of them lie in one device's rows (the rows of one index of rows+grp, 256 consecutive rows), and in every step some device holds exactly 16. `block_inverse`: each step's matrix is symmetric.
All inputs are finite; a program needn't handle non-finite values.
Results may differ from a plain program's by a relative error of at most 0.0001.
Values sent between devices are 32-bit elements; how exact they have to be, the bound alone decides.
A program may use at most 64 MiB of HBM per device.

v0:
```python
import jax
import jax.numpy as jnp
from jax import lax
from jax.sharding import PartitionSpec as P


def gather_turned(arrays, axis, dims):
    turned = [jnp.moveaxis(a, dim, 0) for a, dim in zip(arrays, dims)]
    widths = [t[0].size for t in turned]
    both = jnp.concatenate([t.reshape(-1, w) for t, w in zip(turned, widths)], axis=1)
    filled = lax.all_gather(both, axis, axis=0, tiled=True)
    parts = jnp.split(filled, [sum(widths[:k]) for k in range(1, len(widths))], axis=1)
    return tuple(
        (
            jnp.moveaxis(b.reshape(-1, *t.shape[1:]), 0, dim)
            for b, t, dim in zip(parts, turned, dims)
        )
    )


def joined_along(parts, dim):
    dims = list(parts.shape[1:])
    dims[dim] *= parts.shape[0]
    return jnp.moveaxis(parts, 0, dim).reshape(dims)


def from_everyone(value, axis):
    length = lax.axis_size(axis)
    return lax.all_to_all(
        jnp.broadcast_to(value[None], (length, *value.shape)), axis, 0, 0, tiled=True
    )


def collect(value, axis, dim):
    return joined_along(from_everyone(value, axis), dim)


def kernel_tile(points, others, weights, scale_value):
    weighted = points * weights[:, None]
    cross_terms = lax.dot_general(
        weighted, others, (((0,), (0,)), ((), ())), precision=lax.Precision.HIGHEST
    )
    own_sq = jnp.sum(weighted * points, axis=0)
    other_sq = jnp.sum(others * others * weights[:, None], axis=0)
    return scale_value * jnp.exp(-(own_sq[:, None] + other_sq[None, :] - 2.0 * cross_terms))


def local(
    residual_in,
    solution_in,
    descriptors,
    length_weights,
    amplitude,
    noise,
    block_inverse,
    block_rows,
):
    local_rows = residual_in.shape[0]
    rhs_width = residual_in.shape[1]
    block_size = block_rows.shape[1]
    device_count = lax.axis_size(("rows", "grp"))
    my_index = lax.axis_index(("rows", "grp"))
    slot_count = 4 * block_size // device_count
    positions = jnp.arange(block_size, dtype=jnp.int32)
    residual = residual_in
    solution = solution_in
    for step_index in range(block_rows.shape[0]):
        rows_now = block_rows[step_index]
        owners = rows_now // local_rows
        is_mine = owners == my_index
        local_index = jnp.clip(rows_now - my_index * local_rows, 0, local_rows - 1)
        slot_rank = jnp.cumsum(is_mine.astype(jnp.int32)) - 1
        slot_ids = jnp.arange(slot_count, dtype=jnp.int32)
        picked = is_mine[None, :] & (slot_rank[None, :] == slot_ids[:, None])
        slot_rows = jnp.sum(jnp.where(picked, local_index[None, :], 0), axis=1)
        filled = jnp.any(picked, axis=1)
        send_res = jnp.where(filled[:, None], residual[slot_rows], 0.0)
        send_pts = jnp.where(filled[None, :], descriptors[:, slot_rows], 0.0)
        all_res, all_pts = gather_turned((send_res, send_pts), ("rows", "grp"), (0, 1))
        same_owner = (owners[:, None] == owners[None, :]) & (
            positions[None, :] < positions[:, None]
        )
        owner_rank = jnp.sum(same_owner.astype(jnp.int32), axis=1)
        source = owners * slot_count + owner_rank
        block_res = all_res[source]
        block_points = all_pts[:, source]
        solved_panel = jnp.dot(
            block_inverse[step_index], block_res, precision=lax.Precision.HIGHEST
        )
        empty_rows = jnp.zeros((local_rows, rhs_width), jnp.float32)
        fragment = collect(solved_panel, "grp", 0)
        increment = empty_rows
        kernel_block = kernel_tile(descriptors, block_points, length_weights, amplitude[0])
        kernel_sum = jnp.dot(kernel_block, fragment, precision=lax.Precision.HIGHEST)
        increment = increment.at[local_index].add(jnp.where(is_mine[:, None], fragment, 0.0))
        kernel_sum, increment = (kernel_sum, increment)
        residual = residual - kernel_sum - noise[0] * increment
        solution = solution + increment
    return (solution, residual)


def solution(mesh):
    placed = (
        P(("rows", "grp"), None),
        P(("rows", "grp"), None),
        P(None, ("rows", "grp")),
        P(),
        P(),
        P(),
        P(None, "grp", None),
        P(),
    )
    return jax.shard_map(
        local,
        mesh=mesh,
        in_specs=placed,
        out_specs=(P(("rows", "grp"), None), P(("rows", "grp"), None)),
        check_vma=False,
    )
```

profile of v0, /device:TPU:1, one launch (start us, length us, event | category | flops | bytes accessed | tf_op | source)
XLA Modules:
  0.0 330.9 jit_solution(2361517776596583200)
XLA Ops:
  11.2 1.5 gather_fusion
  19.0 114.0 %all-gather.3.cloned.1.call-done = f32[4096,160]{1,0:T(8,128)} async-done(((f32[16,160]{1,0:T(8,128)}), f32[4096,160]{1,0:T(8,128)}) %all-gather.3.cloned.1.call-update) | async-done | bytes 2621456 | tf_op jit(solution)/shard_map/all_gather | solution.py:11
  133.0 1.6 slice-done
  134.6 2.8 gather_fusion.2
  137.4 2.0 convolution_bitcast_fusion.1
  140.4 4.1 %all-to-all-start = ((f32[8,128,128]{2,1,0:T(8,128)}), f32[8,128,128]{2,1,0:T(8,128)S(1)}, u32[]{:S(2)}, u32[]{:S(2)}) async-start(f32[8,128,128]{2,1,0:T(8,128)} %broadcast_in_dim.136), calls=%async_computation | async-start | bytes 1048576 | tf_op jit(solution)/shard_map/all_to_all | solution.py:29
  144.5 1.7 slice_bitcast_fusion.1
  146.3 2.8 gather_fusion.3
  149.3 1.3 fusion.9
  150.6 11.9 %all-to-all-done = f32[8,128,128]{2,1,0:T(8,128)S(1)} async-done(((f32[8,128,128]{2,1,0:T(8,128)}), f32[8,128,128]{2,1,0:T(8,128)S(1)}, u32[]{:S(2)}, u32[]{:S(2)}) %all-to-all-start) | async-done | bytes 524320 | tf_op jit(solution)/shard_map/all_to_all | solution.py:29
  162.4 8.0 %scatter_custom_fusion = f32[256,128]{1,0:T(8,128)S(1)} fusion(s32[1024]{0:T(1024)S(1)} %bitcast.101, f32[1024,128]{1,0:T(8,128)S(1)} %bitcast.88, f32[]{:T(128)} %constant.44.clone.1, pred[1024]{0:T(1024)(128)(4,1)S(1)} %get-tuple-element.22), kind=kCustom, calls=%fused_computation.40 | custom fusion | flops 262144 | bytes 657408 | tf_op jit(solution)/shard_map/scatter-add | solution.py:95
  170.4 1.9 fusion.11
  173.6 109.7 %all-gather.5.cloned.1.call-done = f32[4096,160]{1,0:T(8,128)} async-done(((f32[16,160]{1,0:T(8,128)}), f32[4096,160]{1,0:T(8,128)}) %all-gather.5.cloned.1.call-update) | async-done | bytes 2621456 | tf_op jit(solution)/shard_map/all_gather | solution.py:11
  283.3 1.6 slice-done.1
  284.9 2.8 gather_fusion.6
  287.7 2.0 convolution_bitcast_fusion
  290.7 4.1 %all-to-all-start.1 = ((f32[8,128,128]{2,1,0:T(8,128)}), f32[8,128,128]{2,1,0:T(8,128)S(1)}, u32[]{:S(2)}, u32[]{:S(2)}) async-start(f32[8,128,128]{2,1,0:T(8,128)} %broadcast_in_dim.143), calls=%async_computation.1 | async-start | bytes 1048576 | tf_op jit(solution)/shard_map/all_to_all | solution.py:29
  294.8 1.7 slice_bitcast_fusion
  296.5 2.8 gather_fusion.7
  299.6 1.3 fusion.5
  300.8 11.9 %all-to-all-done.1 = f32[8,128,128]{2,1,0:T(8,128)S(1)} async-done(((f32[8,128,128]{2,1,0:T(8,128)}), f32[8,128,128]{2,1,0:T(8,128)S(1)}, u32[]{:S(2)}, u32[]{:S(2)}) %all-to-all-start.1) | async-done | bytes 524320 | tf_op jit(solution)/shard_map/all_to_all | solution.py:29
  312.8 8.0 %scatter_custom_fusion.1 = f32[256,128]{1,0:T(8,128)S(1)} fusion(s32[1024]{0:T(1024)S(1)} %bitcast.100, f32[1024,128]{1,0:T(8,128)S(1)} %bitcast.86, f32[]{:T(128)} %constant.44.clone.1, pred[1024]{0:T(1024)(128)(4,1)S(1)} %get-tuple-element.2), kind=kCustom, calls=%fused_computation.37 | custom fusion | flops 262144 | bytes 657408 | tf_op jit(solution)/shard_map/scatter-add | solution.py:95
  320.8 1.6 add_add_fusion
  322.4 1.7 fusion.10
  (54 shorter events, 12.6 us)
Async XLA Ops:
  7.2 125.8 %all-gather.3.cloned.1.call-start = ((), (), s32[]{:S(2)}) async-start(), calls=%async_computation.2 | async-start | bytes 4210688 | tf_op jit(solution)/shard_map/all_gather | solution.py:11
  133.0 1.6 slice-start
  137.4 11.7 %copy-start.1 = (f32[32]{0:T(128)S(1)}, f32[32]{0:T(128)}, u32[]{:S(2)}) copy-start(f32[32]{0:T(128)} %param.11) | copy-start | bytes 388
  137.4 11.9 %copy-start = (f32[32,256]{1,0:T(8,128)S(1)}, f32[32,256]{1,0:T(8,128)}, u32[]{:S(2)}) copy-start(f32[32,256]{1,0:T(8,128)} %param.10) | copy-start | bytes 98308
  140.4 22.1 %all-to-all-start = ((f32[8,128,128]{2,1,0:T(8,128)}), f32[8,128,128]{2,1,0:T(8,128)S(1)}, u32[]{:S(2)}, u32[]{:S(2)}) async-start(f32[8,128,128]{2,1,0:T(8,128)} %broadcast_in_dim.136), calls=%async_computation | async-start | bytes 1048576 | tf_op jit(solution)/shard_map/all_to_all | solution.py:29
  144.5 138.8 %all-gather.5.cloned.1.call-start = ((), (), s32[]{:S(2)}) async-start(), calls=%async_computation.3 | async-start | bytes 4210688 | tf_op jit(solution)/shard_map/all_gather | solution.py:11
  283.3 1.6 slice-start.1
  290.7 22.1 %all-to-all-start.1 = ((f32[8,128,128]{2,1,0:T(8,128)}), f32[8,128,128]{2,1,0:T(8,128)S(1)}, u32[]{:S(2)}, u32[]{:S(2)}) async-start(f32[8,128,128]{2,1,0:T(8,128)} %broadcast_in_dim.143), calls=%async_computation.1 | async-start | bytes 1048576 | tf_op jit(solution)/shard_map/all_to_all | solution.py:29
Sparse Core Ops, SparseCore 0:
  13.5 119.3 all-gather.2
  173.7 109.5 all-gather.4
where the time goes:
time: 332 us; the launch traced here: 331 us
  waiting for transfers between devices  248 us (75%)
  other arithmetic  25.3 us (8%)
  local copies, waits for them, and re-layouts  24.1 us (7%)
  between operations  15.6 us (5%)
  matrix products  10.1 us (3%)
  starting transfers between devices  8.31 us (3%)
    all_gather x2, waiting for transfers between devices, gather_turned(): filled = lax.all_gather(both, axis, axis=0, tiled=True)  224 us
    all_to_all x2, waiting for transfers between devices, from_everyone(): lax.all_to_all(jnp.broadcast_to(value[None], (length, *value.shape)), axi...  23.8 us
    scatter-add x2, other arithmetic, local(): increment.at[local_index].add(jnp.where(is_mine[:, None], fragment, 0.0))  16 us
    all_to_all x2, starting transfers between devices, from_everyone(): lax.all_to_all(jnp.broadcast_to(value[None], (length, *value.shape)), axi...  8.23 us
  transfers between devices with their start and end apart: 4, of which 4 were waited for; matrix products, arithmetic and copies ran while one was open for 5% of the time, Pallas kernels for 0%

commit v1 on v0

v1 whole, which is shorter than its diff:
```python
import jax
import jax.numpy as jnp
from jax import lax
from jax.experimental import pallas as pl
from jax.experimental.pallas import tpu as pltpu
from jax.sharding import PartitionSpec as P

MESH = pl.DeviceIdType.MESH
F32 = jnp.float32
BF16 = jnp.bfloat16
EXACT = lax.Precision.HIGHEST
LINES, DEPTH, CHIPS, HALF = 32, 8, 16, 4
NT = (((1,), (1,)), ((), ()))
TN = (((0,), (0,)), ((), ()))


def iota(shape, dim):
    return lax.broadcasted_iota(jnp.int32, shape, dim)


def dot(a, b, dims=(((1,), (0,)), ((), ()))):
    return lax.dot_general(a, b, dims, preferred_element_type=F32)


def parts2(x):
    high = x.astype(BF16).astype(F32)
    return high, x - high


def parts3(x):
    high = x.astype(BF16).astype(F32)
    rest = x - high
    middle = rest.astype(BF16).astype(F32)
    return high, middle, rest - middle


def stack2(x):
    return jnp.concatenate(parts2(x), axis=0).astype(BF16)


def stack3(x):
    return jnp.concatenate(parts3(x), axis=0).astype(BF16)


def left_side(points, weights):
    n = points.shape[1]
    w = weights[:, :1]
    a1, a2, a3 = parts3(2.0 * (w * points))
    s1, s2, s3 = parts3(-jnp.sum(w * points * points, axis=0, keepdims=True))
    row = iota((16, n), 0)
    tail = jnp.where(row == 0, s1, jnp.where(row == 1, s2, jnp.where(row == 2, s3, jnp.where(row < 6, 1.0, 0.0))))
    return jnp.concatenate([a1, a1, a2, a1, a2, a3, tail], axis=0).astype(BF16)


def right_side(points, weights):
    n = points.shape[1]
    w = weights[:, :1]
    b1, b2, b3 = parts3(points)
    s1, s2, s3 = parts3(-jnp.sum(w * points * points, axis=0, keepdims=True))
    row = iota((16, n), 0)
    tail = jnp.where(row < 3, 1.0, jnp.where(row == 3, s1, jnp.where(row == 4, s2, jnp.where(row == 5, s3, 0.0))))
    return jnp.concatenate([b1, b2, b1, b3, b2, b1, tail], axis=0).astype(BF16)


def small_product(x, split_matrix):
    n = split_matrix.shape[0] // 2
    out = dot(stack2(x), split_matrix, NT)
    return out[:8, :n] + out[8:, :n] + out[:8, n:]


def kernel(
    res_ref, sol_ref, desc_ref, inv_ref, rows_ref, w_ref, amp_ref, noise_ref,
    sol_out, res_out,
    cols, ids, onehot, lines, tiles, slots, points_in, part_out, part_in, right, left,
    invs, ag, solved, spread, kern,
    s_line, r_line, s_tile, r_tile, s_pts, r_pts, s_part, r_part,
    s_solved, r_solved, s_spread, r_spread, s_fwd, r_fwd,
):
    r = lax.axis_index("rows")
    z = lax.axis_index("grp")
    chip, core = lax.div(r, 2), lax.rem(r, 2)
    sibling = r + 1 - 2 * core
    base = (r * DEPTH + z) * 256
    amp = amp_ref[0]
    noise = noise_ref[0]

    barrier = pltpu.get_barrier_semaphore()

    def greet_depth(k, carry):
        pl.semaphore_signal(barrier, inc=1, device_id=(r, lax.rem(z + k, DEPTH)), device_id_type=MESH)
        return carry

    def greet_plane(k, carry):
        pl.semaphore_signal(barrier, inc=1, device_id=(lax.rem(r + k, LINES), z), device_id_type=MESH)
        return carry

    lax.fori_loop(1, DEPTH, greet_depth, 0)
    lax.fori_loop(1, LINES, greet_plane, 0)

    weights = jnp.zeros((32, 128), F32)
    for d in range(32):
        weights = jnp.where(iota((32, 128), 0) == d, w_ref[d], weights)
    picks = []
    lane = iota((1, 256), 1)
    before = (iota((256, 256), 0) < iota((256, 256), 1)).astype(F32).astype(BF16)
    for s in range(2):
        for k in range(8):
            row = rows_ref[s:s + 1, 128 * k:128 * k + 128].astype(F32)
            cols[s, 128 * k:128 * k + 128, :] = jnp.broadcast_to(row, (128, 128)).T
        member = []
        for h in range(2):
            here = (base + 128 * h + iota((1, 128), 1)).astype(F32)
            hit = jnp.where(cols[s] == here, 1.0, 0.0)
            member.append(jnp.max(hit, axis=0, keepdims=True))
        member = jnp.concatenate(member, axis=1)
        rank = dot(jnp.broadcast_to(member, (16, 256)).astype(BF16), before)
        slot = iota((16, 256), 0).astype(F32)
        picks.append(jnp.where((rank == slot) & (member > 0.5), 1.0, 0.0))
    picks = jnp.concatenate(picks, axis=0)
    picked_res = jnp.dot(picks, res_ref[...], precision=EXACT)
    desc = desc_ref[...]
    picked_pts = lax.dot_general(
        picks, jnp.concatenate([desc] * 4, axis=0), NT, precision=EXACT
    )
    quarter = lax.div(iota((8, 128), 1), 32)
    packed = jnp.zeros((8, 128), F32)
    for q in range(4):
        packed = jnp.where(quarter == q, picked_pts[8 * q:8 * q + 8], packed)
    lines[z] = jnp.concatenate([picked_res, packed], axis=0)

    pl.semaphore_wait(barrier, DEPTH - 1 + LINES - 1)

    def line_copy(k):
        return pltpu.make_async_remote_copy(
            src_ref=lines.at[z], dst_ref=lines.at[z], send_sem=s_line.at[k], recv_sem=r_line.at[k],
            device_id=(r, lax.rem(z + k, DEPTH)), device_id_type=MESH)

    for k in range(1, DEPTH):
        line_copy(k).start()

    for s in range(2):
        invs[s] = stack2(inv_ref[s])

    def slot_ids(s):
        rows = rows_ref[s:s + 1, :]
        owner = lax.shift_right_logical(rows, 8)
        first = (owner * 256).astype(F32)
        value = rows.astype(F32)

        def count(q, total):
            col = cols[s, pl.ds(pl.multiple_of(q * 128, 128), 128), :]
            out = []
            for k in range(8):
                cut = slice(128 * k, 128 * k + 128)
                hit = (col >= first[:, cut]) & (col < value[:, cut])
                out.append(jnp.sum(jnp.where(hit, 1.0, 0.0).reshape(16, 8, 128), axis=0))
            return total + jnp.concatenate(out, axis=1)

        total = lax.fori_loop(0, 8, count, jnp.zeros((8, 1024), F32))
        rank = jnp.sum(total, axis=0, keepdims=True).astype(jnp.int32)
        line = lax.shift_right_logical(owner, 3)
        ids[s:s + 1, :] = (
            (line & 1) * 2048 + lax.shift_right_logical(line, 1) * 128
            + lax.shift_right_logical(rank, 3) * 64 + (owner & 7) * 8 + (rank & 7))

    def fill_onehot(s):
        def fill(k, carry):
            for c in range(2):
                want = ids[s:s + 1, :] - (c * 2048 + k * 128)
                onehot[s, c, pl.ds(pl.multiple_of(k * 128, 128), 128), :] = jnp.where(
                    iota((128, 1024), 0) == want, 1.0, 0.0).astype(BF16)
            return carry
        lax.fori_loop(0, CHIPS, fill, 0)

    slot_ids(0)
    fill_onehot(0)

    for k in range(1, DEPTH):
        line_copy(k).wait_recv()

    turned = []
    for s in range(2):
        turned.append(jnp.concatenate(
            [lines[:, 16 * s + 8 * h:16 * s + 8 * h + 8, :].reshape(64, 128) for h in range(2)], axis=0).T)
    t0, t1 = (t.reshape(16, 8, 128) for t in turned)
    upper = iota((16, 8, 128), 1) < 4
    tiles[:, 0] = jnp.where(upper, t0, pltpu.roll(t1, 4, 1))
    tiles[:, 1] = jnp.where(upper, pltpu.roll(t0, 4, 1), t1)

    def tile_copy(k):
        to = lax.rem(r + k, LINES)
        return pltpu.make_async_remote_copy(
            src_ref=tiles.at[lax.div(to, 2), lax.rem(to, 2)], dst_ref=slots.at[core, chip],
            send_sem=s_tile.at[k], recv_sem=r_tile.at[k], device_id=(to, z), device_id_type=MESH)

    def start_tile(k, carry):
        tile_copy(k).start()
        return carry

    lax.fori_loop(1, LINES, start_tile, 0)
    slots[core, chip] = tiles[chip, core]

    a = lines[:, 32:40, :].reshape(64, 128)
    turned = jnp.concatenate([a, pltpu.roll(a, 96, 1)], axis=0).T
    points_in[chip] = jnp.concatenate([turned[:32], turned[64:96]], axis=0)

    def points_copy(k):
        return pltpu.make_async_remote_copy(
            src_ref=points_in.at[chip], dst_ref=points_in.at[chip], send_sem=s_pts.at[k], recv_sem=r_pts.at[k],
            device_id=(lax.rem(r + 2 * k, LINES), z), device_id_type=MESH)

    def start_points(k, carry):
        points_copy(k).start()
        return carry

    lax.fori_loop(1, CHIPS, start_points, 0)

    slot_ids(1)
    fill_onehot(1)
    left_own = left_side(desc, weights)

    def wait_tile(k, carry):
        tile_copy(k).wait_recv()
        return carry

    lax.fori_loop(1, LINES, wait_tile, 0)

    halves = [
        stack3(jnp.concatenate([slots[c, k] for k in range(CHIPS)], axis=1)) for c in range(2)
    ]

    def ordered(s):
        out = dot(halves[0], onehot[s, 0]) + dot(halves[1], onehot[s, 1])
        return out[:8] + out[8:16] + out[16:]

    def solved_copy(s, k):
        return pltpu.make_async_remote_copy(
            src_ref=solved.at[s, z], dst_ref=solved.at[s, z], send_sem=s_solved.at[s, k], recv_sem=r_solved.at[s, k],
            device_id=(r, lax.rem(z + k, DEPTH)), device_id_type=MESH)

    solved[0, z] = small_product(ordered(0), invs[0])
    for k in range(1, DEPTH):
        solved_copy(0, k).start()

    panel1 = small_product(pltpu.roll(ordered(1), 4, 0), invs[1])

    def wait_points(k, carry):
        points_copy(k).wait_recv()
        return carry

    lax.fori_loop(1, CHIPS, wait_points, 0)
    for s in range(2):
        block = jnp.concatenate([points_in[k, 32 * s:32 * s + 32] for k in range(CHIPS)], axis=1)
        out = dot(stack3(block), onehot[s, core])
        part_out[32 * s:32 * s + 32] = out[:32] + out[32:64] + out[64:]
    part = pltpu.make_async_remote_copy(
        src_ref=part_out, dst_ref=part_in, send_sem=s_part, recv_sem=r_part,
        device_id=(sibling, z), device_id_type=MESH)
    part.start()
    part.wait_recv()
    block_points = part_out[...] + part_in[...]
    for s in range(2):
        right[s] = right_side(block_points[32 * s:32 * s + 32], weights)
    left[...] = left_side(block_points[32:64], weights)

    total = jnp.zeros((128, 1024), F32)
    for k in range(4):
        cut = slice(256 * k, 256 * k + 256)
        tile = amp * jnp.exp(dot(left[:, cut], right[0], TN))
        rows0 = rows_ref[0:1, :].astype(F32)
        same = jnp.concatenate(
            [cols[1, cut, :] == rows0[:, 128 * m:128 * m + 128] for m in range(8)], axis=1)
        tile = tile + jnp.where(same, noise, 0.0)
        high, low = parts2(tile)
        out = dot(invs[1, :, cut], high.astype(BF16))
        total = total + out[:128] + out[128:] + dot(invs[1, :128, cut], low.astype(BF16))
    ag[...] = stack2(total)

    for k in range(1, DEPTH):
        solved_copy(0, k).wait_recv()

    def whole(s):
        return jnp.concatenate([solved[s, k] for k in range(DEPTH)], axis=1)

    def spread_copy(s, k):
        return pltpu.make_async_remote_copy(
            src_ref=spread.at[s, core, chip], dst_ref=spread.at[s, core, chip],
            send_sem=s_spread.at[s, k], recv_sem=r_spread.at[s, k],
            device_id=(lax.rem(r + 2 * k, LINES), z), device_id_type=MESH)

    def forward_copy(s, k):
        origin = lax.rem(chip + CHIPS - k, CHIPS)
        return pltpu.make_async_remote_copy(
            src_ref=spread.at[s, core, origin], dst_ref=spread.at[s, core, origin],
            send_sem=s_fwd.at[s, k], recv_sem=r_fwd.at[s, k],
            device_id=(sibling, z), device_id_type=MESH)

    def spread_out(s, mine):
        spread[s, core, chip] = jnp.where(
            iota((8, 512), 0) < 4, mine[:, :512], pltpu.roll(mine[:, 512:], 4, 0))

        def start(k, carry):
            spread_copy(s, k).start()
            return carry

        lax.fori_loop(1, CHIPS, start, 0)
        forward_copy(s, 0).start()

    def pass_on(s):
        def step(k, carry):
            spread_copy(s, k).wait_recv()
            forward_copy(s, k).start()
            return carry

        lax.fori_loop(1, CHIPS, step, 0)

    first = whole(0)
    solved[1, z] = panel1 - small_product(first, ag[...])
    for k in range(1, DEPTH):
        solved_copy(1, k).start()
    spread_out(0, first)

    for s in range(2):
        high, low = parts2(amp * jnp.exp(dot(left_own, right[s], TN)))
        kern[s, :256] = high.astype(BF16)
        kern[s, 256:512] = low.astype(BF16)
        own = iota((256, 1024), 0) + base == rows_ref[s:s + 1, :]
        kern[s, 512:] = jnp.where(own, 1.0, 0.0).astype(BF16)

    for k in range(1, DEPTH):
        solved_copy(1, k).wait_recv()
    spread_out(1, whole(1))

    def change(s):
        def wait(k, carry):
            forward_copy(s, k).wait_recv()
            return carry

        lax.fori_loop(0, CHIPS, wait, 0)
        even, odd = spread[s, 0], spread[s, 1]
        top = iota((CHIPS, 8, 512), 1) < 4
        update = jnp.concatenate([
            jnp.where(top, even, pltpu.roll(odd, 4, 1)).reshape(128, 512),
            jnp.where(top, pltpu.roll(even, 4, 1), odd).reshape(128, 512)], axis=1)
        out = dot(kern[s], stack2(update), NT)
        smooth = out[:256, :128] + out[:256, 128:] + out[256:512, :128]
        return smooth, out[512:, :128] + out[512:, 128:]

    pass_on(0)
    smooth0, own0 = change(0)
    pass_on(1)
    smooth1, own1 = change(1)
    moved = own0 + own1
    sol_out[...] = sol_ref[...] + moved
    res_out[...] = res_ref[...] - smooth0 - smooth1 - noise * moved

    for k in range(1, DEPTH):
        line_copy(k).wait_send()
        for s in range(2):
            solved_copy(s, k).wait_send()

    def drain_tiles(k, carry):
        tile_copy(k).wait_send()
        return carry

    def drain_chips(k, carry):
        points_copy(k).wait_send()
        for s in range(2):
            spread_copy(s, k).wait_send()
            forward_copy(s, k).wait_send()
        return carry

    lax.fori_loop(1, LINES, drain_tiles, 0)
    lax.fori_loop(1, CHIPS, drain_chips, 0)
    for s in range(2):
        forward_copy(s, 0).wait_send()
    part.wait_send()


def local(residual_in, solution_in, descriptors, length_weights, amplitude, noise, block_inverse, block_rows):
    vmem = pl.BlockSpec(memory_space=pltpu.VMEM)
    smem = pl.BlockSpec(memory_space=pltpu.SMEM)
    dma = pltpu.SemaphoreType.DMA
    shape = jax.ShapeDtypeStruct(residual_in.shape, F32)
    return pl.pallas_call(
        kernel,
        out_shape=(shape, shape),
        in_specs=[vmem] * 5 + [smem] * 3,
        out_specs=(vmem, vmem),
        scratch_shapes=[
            pltpu.VMEM((2, 1024, 128), F32),
            pltpu.VMEM((2, 1024), jnp.int32),
            pltpu.VMEM((2, 2, 2048, 1024), BF16),
            pltpu.VMEM((DEPTH, 40, 128), F32),
            pltpu.VMEM((CHIPS, 2, 8, 128), F32),
            pltpu.VMEM((2, CHIPS, 8, 128), F32),
            pltpu.VMEM((CHIPS, 64, 128), F32),
            pltpu.VMEM((64, 1024), F32),
            pltpu.VMEM((64, 1024), F32),
            pltpu.VMEM((2, 208, 1024), BF16),
            pltpu.VMEM((208, 1024), BF16),
            pltpu.VMEM((2, 256, 1024), BF16),
            pltpu.VMEM((256, 1024), BF16),
            pltpu.VMEM((2, DEPTH, 8, 128), F32),
            pltpu.VMEM((2, 2, CHIPS, 8, 512), F32),
            pltpu.VMEM((2, 768, 1024), BF16),
            dma((DEPTH,)), dma((DEPTH,)), dma((LINES,)), dma((LINES,)), dma((CHIPS,)), dma((CHIPS,)),
            dma, dma,
            dma((2, DEPTH)), dma((2, DEPTH)), dma((2, CHIPS)), dma((2, CHIPS)), dma((2, CHIPS)), dma((2, CHIPS)),
        ],
        compiler_params=pltpu.CompilerParams(
            collective_id=0, has_side_effects=True, vmem_limit_bytes=56 * 1024 * 1024),
    )(residual_in, solution_in, descriptors, block_inverse, block_rows, length_weights, amplitude, noise)


def solution(mesh):
    placed = (
        P(("rows", "grp"), None),
        P(("rows", "grp"), None),
        P(None, ("rows", "grp")),
        P(),
        P(),
        P(),
        P(None, "grp", None),
        P(),
    )
    return jax.shard_map(
        local,
        mesh=mesh,
        in_specs=placed,
        out_specs=(P(("rows", "grp"), None), P(("rows", "grp"), None)),
        check_vma=False,
    )
```

time: 332 us -> 54.5 us (0.16)
  waiting for transfers between devices: 248 us -> 0 us
  Pallas kernels: 0 us -> 50.2 us
  other arithmetic: 25.3 us -> 0 us
  local copies, waits for them, and re-layouts: 24.1 us -> 2.26 us
  between operations: 15.6 us -> 1.94 us
  matrix products: 10.1 us -> 0 us
  starting transfers between devices: 8.31 us -> 0 us
    all_gather x2 -> x0, waiting for transfers between devices: 224 us -> none  [gather_turned(): filled = lax.all_gather(both, axis, axis=0, tiled=True)]
    pallas_call x0 -> x1, Pallas kernels: none -> 50.2 us  [local(): pl.pallas_call(kernel, out_shape=(shape, shape), in_specs=[vmem] * 5 + [s...]
    all_to_all x2 -> x0, waiting for transfers between devices: 23.8 us -> none  [from_everyone(): lax.all_to_all(jnp.broadcast_to(value[None], (length, *value.shape)), axi...]
    scatter-add x2 -> x0, other arithmetic: 16 us -> none  [local(): increment.at[local_index].add(jnp.where(is_mine[:, None], fragment, 0.0))]
    gather x8 -> x0, local copies, waits for them, and re-layouts: 14.4 us -> none  [the longest x2 5.62 us: local(): block_points = all_pts[:, source]]
    dot_general x6 -> x0, matrix products: 10.1 us -> none  [the longest x2 4.07 us: local(): jnp.dot(block_inverse[step_index], block_res, precision=lax.Precision.HIG...]
    all_to_all x2 -> x0, starting transfers between devices: 8.23 us -> none  [from_everyone(): lax.all_to_all(jnp.broadcast_to(value[None], (length, *value.shape)), axi...]
    transpose x2 -> x0, local copies, waits for them, and re-layouts: 3.45 us -> none  [gather_turned(): jnp.moveaxis(b.reshape(-1, *t.shape[1:]), 0, dim)]
  transfers between devices with their start and end apart: 4 -> 0, of which waited for: 4 -> 0; matrix products, arithmetic and copies ran while one was open for 5% -> 0% of each run, Pallas kernels for 0% -> 0%
where the time goes in v1:
time: 54.5 us; the launch traced here: 54.4 us
  Pallas kernels  50.2 us (92%)
  local copies, waits for them, and re-layouts  2.26 us (4%)
  between operations  1.94 us (4%)
    pallas_call x1, Pallas kernels, local(): pl.pallas_call(kernel, out_shape=(shape, shape), in_specs=[vmem] * 5 + [s...  50.2 us
    unnamed x4, local copies, waits for them, and re-layouts  2.26 us

profile of v1, /device:TPU:1, one launch (start us, length us, event | category | flops | bytes accessed | tf_op | source)
XLA Modules:
  0.0 54.4 jit_solution(6013740227414618860)
XLA Ops:
  1.9 50.2 %shard_map.95 = (f32[256,128]{1,0:T(8,128)}, f32[256,128]{1,0:T(8,128)}) custom-call(f32[256,128]{1,0:T(8,128)} %res_ref.1, f32[256,128]{1,0:T(8,128)} %sol_ref.1, f32[32,256]{1,0:T(8,128)} %desc_ref.1, f32[2,128,1024]{2,1,0:T(8,128)} %inv_ref.1, s32[2,1024]{1,0:T(2,128)} %rows_ref.1, f32[32]{0:T(128)} %w_ref.1, f32[1]{0:T(128)S(6)} %copy.12.amp_ref, ...), custom_call_target="tpu_custom_call" | custom-call | tf_op jit(solution)/shard_map/pallas_call | solution.py:385
  52.1 0.0 copy-start
  52.1 1.6 %copy.14 = f32[256,128]{1,0:T(8,128)} copy(f32[256,128]{1,0:T(8,128)} %get-tuple-element.4) | data formatting | bytes 262144
  53.7 0.0 copy-done
  53.8 0.7 %copy.15 = f32[256,128]{1,0:T(8,128)} copy(f32[256,128]{1,0:T(8,128)S(1)} %copy-done) | data formatting | bytes 262144
Async XLA Ops:
  52.1 1.6 %copy-start = (f32[256,128]{1,0:T(8,128)S(1)}, f32[256,128]{1,0:T(8,128)}, u32[]{:S(2)}) copy-start(f32[256,128]{1,0:T(8,128)} %get-tuple-element.5) | copy-start | bytes 393220

commit v2 on v1

v2 whole, which is shorter than its diff:
```python
import jax
import jax.numpy as jnp
from jax import lax
from jax.experimental import pallas as pl
from jax.experimental.pallas import tpu as pltpu
from jax.sharding import PartitionSpec as P

MESH = pl.DeviceIdType.MESH
F32 = jnp.float32
BF16 = jnp.bfloat16
LINES, DEPTH, CHIPS = 32, 8, 16
FAR_FIRST = (4, 3, 5, 2, 6, 1, 7)
OFFSETS = sorted(
    ((a, b) for a in range(4) for b in range(4) if a or b),
    key=lambda o: -(min(o[0], 4 - o[0]) + min(o[1], 4 - o[1])))
GROUPS = (OFFSETS[:5], OFFSETS[5:10], OFFSETS[10:])
VMEM_BYTES = 56 * 1024 * 1024
NT = (((1,), (1,)), ((), ()))
TN = (((0,), (0,)), ((), ()))


def iota(shape, dim):
    return lax.broadcasted_iota(jnp.int32, shape, dim)


def dot(a, b, dims=(((1,), (0,)), ((), ()))):
    return lax.dot_general(a, b, dims, preferred_element_type=F32)


def parts2(x):
    high = x.astype(BF16).astype(F32)
    return high, x - high


def parts3(x):
    high = x.astype(BF16).astype(F32)
    rest = x - high
    middle = rest.astype(BF16).astype(F32)
    return high, middle, rest - middle


def stack2(x):
    return jnp.concatenate(parts2(x), axis=0).astype(BF16)


def stack3(x):
    return jnp.concatenate(parts3(x), axis=0).astype(BF16)


def left_side(points, weights, log_amp):
    n = points.shape[1]
    w = weights[:, :1]
    a1, a2, a3 = parts3(2.0 * (w * points))
    s1, s2, s3 = parts3(log_amp - jnp.sum(w * points * points, axis=0, keepdims=True))
    row = iota((16, n), 0)
    tail = jnp.where(row == 0, s1, jnp.where(row == 1, s2, jnp.where(row == 2, s3, jnp.where(row < 6, 1.0, 0.0))))
    return jnp.concatenate([a1, a1, a2, a1, a2, a3, tail], axis=0).astype(BF16)


def right_side(points, weights):
    n = points.shape[1]
    w = weights[:, :1]
    b1, b2, b3 = parts3(points)
    s1, s2, s3 = parts3(-jnp.sum(w * points * points, axis=0, keepdims=True))
    row = iota((16, n), 0)
    tail = jnp.where(row < 3, 1.0, jnp.where(row == 3, s1, jnp.where(row == 4, s2, jnp.where(row == 5, s3, 0.0))))
    return jnp.concatenate([b1, b2, b1, b3, b2, b1, tail], axis=0).astype(BF16)


def small_product(x, split_matrix):
    n = split_matrix.shape[0] // 2
    out = dot(stack2(x), split_matrix, NT)
    return out[:8, :n] + out[8:, :n] + out[:8, n:]


def kernel(
    res_hbm, sol_hbm, desc_hbm, inv_hbm, rows_hbm, w_hbm, amp_hbm, noise_hbm,
    sol_out, res_out,
    res_ref, sol_ref, desc_ref, inv_ref, rows_ref, w_ref, amp_ref, noise_ref,
    cols, ids, onehot, lines, packs, tiles, slots, points_in, part_out, part_in, right, left,
    invs, inv_slots, noisy, ag, solved, spread, kern, load_sem, late_sem,
    s_line, r_line, s_pack, r_pack, s_tile, r_tile, s_pts, r_pts, s_part, r_part,
    s_solved, r_solved, s_spread, r_spread, s_fwd, r_fwd,
):
    r = lax.axis_index("rows")
    z = lax.axis_index("grp")
    chip, core = lax.div(r, 2), lax.rem(r, 2)
    sibling = r + 1 - 2 * core
    base = (r * DEPTH + z) * 256

    loads = [
        pltpu.make_async_copy(a, b, load_sem.at[k])
        for k, (a, b) in enumerate([
            (rows_hbm, rows_ref), (res_hbm, res_ref), (desc_hbm, desc_ref), (w_hbm, w_ref),
            (amp_hbm, amp_ref), (noise_hbm, noise_ref)])]
    late = [
        pltpu.make_async_copy(a, b, late_sem.at[k])
        for k, (a, b) in enumerate([(inv_hbm, inv_ref), (sol_hbm, sol_ref)])]
    for copy in loads + late:
        copy.start()
    barrier = pltpu.get_barrier_semaphore()

    def greet_depth(k, carry):
        for line in (r, sibling):
            pl.semaphore_signal(barrier, inc=1, device_id=(line, lax.rem(z + k, DEPTH)), device_id_type=MESH)
        return carry

    def greet_plane(k, carry):
        pl.semaphore_signal(barrier, inc=1, device_id=(lax.rem(r + k, LINES), z), device_id_type=MESH)
        return carry

    lax.fori_loop(1, DEPTH, greet_depth, 0)
    lax.fori_loop(1, LINES, greet_plane, 0)
    for copy in loads[:2]:
        copy.wait()
    before = (iota((256, 256), 0) < iota((256, 256), 1)).astype(F32).astype(BF16)

    def pick(s):
        for k in range(8):
            row = rows_ref[s:s + 1, 128 * k:128 * k + 128].astype(F32)
            cols[s, 128 * k:128 * k + 128, :] = jnp.broadcast_to(row, (128, 128)).T
        member = []
        for h in range(2):
            here = (base + 128 * h + iota((1, 128), 1)).astype(F32)
            hit = jnp.where(cols[s] == here, 1.0, 0.0)
            member.append(jnp.max(hit, axis=0, keepdims=True))
        member = jnp.concatenate(member, axis=1)
        rank = dot(jnp.broadcast_to(member, (16, 256)).astype(BF16), before)
        slot = iota((16, 256), 0).astype(F32)
        mine = jnp.where((rank == slot) & (member > 0.5), 1.0, 0.0).astype(BF16)
        out = dot(mine, split_res)
        lines[s, z] = out[:, :128] + out[:, 128:256] + out[:, 256:]
        return mine

    split_res = jnp.concatenate(parts3(res_ref[...]), axis=1).astype(BF16)
    picks = [pick(0)]
    pl.semaphore_wait(barrier, 2 * (DEPTH - 1) + LINES - 1)

    def remote(src, dst, send, recv, to):
        return pltpu.make_async_remote_copy(
            src_ref=src, dst_ref=dst, send_sem=send, recv_sem=recv, device_id=to, device_id_type=MESH)

    def along(k):
        return (r, lax.rem(z + k, DEPTH))

    def line_copy(s, k):
        return remote(lines.at[s, z], lines.at[s, z], s_line.at[s], r_line.at[s], along(k))

    def all_lines(s):
        return remote(lines.at[s, 0:DEPTH - 1], lines.at[s, 0:DEPTH - 1], s_line.at[s], r_line.at[s], along(1))

    def pack_copy(k):
        return remote(packs.at[z], packs.at[z], s_pack, r_pack, along(k))

    all_packs = remote(packs.at[0:DEPTH - 1], packs.at[0:DEPTH - 1], s_pack, r_pack, along(1))

    for k in FAR_FIRST:
        line_copy(0, k).start()
    picks.append(pick(1))
    for copy in loads[2:]:
        copy.wait()
    noise = noise_ref[0]
    weights = jnp.zeros((32, 128), F32)
    for d in range(32):
        weights = jnp.where(iota((32, 128), 0) == d, w_ref[d], weights)
    log_amp = jnp.log(jnp.broadcast_to(amp_ref[0], (1, 128)))[:, :1]
    desc = desc_ref[...]
    wide = jnp.concatenate([part for part in parts3(desc) for _ in range(4)], axis=0).astype(BF16)
    out = jnp.concatenate([dot(mine, wide, NT) for mine in picks], axis=0)
    picked_pts = out[:, :128] + out[:, 128:256] + out[:, 256:]
    quarter = lax.div(iota((8, 128), 1), 32)
    packed = jnp.zeros((8, 128), F32)
    for q in range(4):
        packed = jnp.where(quarter == q, picked_pts[8 * q:8 * q + 8], packed)
    packs[z] = packed
    for k in FAR_FIRST:
        pack_copy(k).start()
    for k in FAR_FIRST:
        line_copy(1, k).start()

    late[0].wait()
    for s in range(2):
        invs[s] = stack2(inv_ref[s])

    def slot_ids(s):
        rows = rows_ref[s:s + 1, :]
        owner = lax.shift_right_logical(rows, 8)
        first = (owner * 256).astype(F32)
        value = rows.astype(F32)

        def count(q, total):
            col = cols[s, pl.ds(pl.multiple_of(q * 128, 128), 128), :]
            out = []
            for k in range(8):
                cut = slice(128 * k, 128 * k + 128)
                hit = (col >= first[:, cut]) & (col < value[:, cut])
                out.append(jnp.sum(jnp.where(hit, 1.0, 0.0).reshape(16, 8, 128), axis=0))
            return total + jnp.concatenate(out, axis=1)

        total = lax.fori_loop(0, 8, count, jnp.zeros((8, 1024), F32))
        rank = jnp.sum(total, axis=0, keepdims=True).astype(jnp.int32)
        line = lax.shift_right_logical(owner, 3)
        ids[s:s + 1, :] = (
            (line & 1) * 2048 + lax.shift_right_logical(line, 1) * 128
            + lax.shift_right_logical(rank, 3) * 64 + (owner & 7) * 8 + (rank & 7))

    def fill_onehot(s):
        def fill(k, carry):
            want = ids[s:s + 1, :] - (core * 2048 + k * 128)
            onehot[s, pl.ds(pl.multiple_of(k * 128, 128), 128), :] = jnp.where(
                iota((128, 1024), 0) == want, 1.0, 0.0).astype(BF16)
            return carry
        lax.fori_loop(0, CHIPS, fill, 0)

    slot_ids(0)
    fill_onehot(0)

    def make_tiles(s):
        tiles[s] = jnp.concatenate(
            [lines[s, :, 8 * h:8 * h + 8, :].reshape(64, 128) for h in range(2)], axis=0).T.reshape(CHIPS, 8, 128)

    def shifted(offset, sign=1):
        a, b = offset
        x, y = lax.div(chip, 4), lax.rem(chip, 4)
        return lax.rem(x + 4 + sign * a, 4) * 4 + lax.rem(y + 4 + sign * b, 4)

    def tile_copy(s, to):
        return remote(tiles.at[s, to], slots.at[s, chip], s_tile.at[s], r_tile.at[s], (2 * to + core, z))

    def all_tiles(s):
        return remote(slots.at[s, 0:CHIPS - 1], slots.at[s, 0:CHIPS - 1], s_tile.at[s], r_tile.at[s], (sibling, z))

    def send_tiles(s):
        for offset in OFFSETS:
            tile_copy(s, shifted(offset)).start()
        slots[s, chip] = tiles[s, chip]

    def across(offset):
        return (2 * shifted(offset) + core, z)

    side = lax.div(chip, 8)

    def points_copy(k):
        return remote(points_in.at[chip], points_in.at[chip], s_pts, r_pts.at[side], across(k))

    def some_points(n, h):
        return remote(points_in.at[0:n], points_in.at[0:n], s_pts, r_pts.at[h], (sibling, z))

    all_lines(0).wait_recv()
    make_tiles(0)
    send_tiles(0)
    all_packs.wait_recv()
    a = packs[...].reshape(64, 128)
    turned = jnp.concatenate([a, pltpu.roll(a, 96, 1)], axis=0).T
    points_in[chip] = jnp.concatenate([turned[:32], turned[64:96]], axis=0)
    for offset in OFFSETS:
        points_copy(offset).start()
    all_lines(1).wait_recv()
    make_tiles(1)
    send_tiles(1)

    inv_slots[...] = dot(invs[0], onehot[0], NT).astype(BF16)
    slot_ids(1)
    fill_onehot(1)
    first_row = pl.multiple_of(512 * core, 512)
    mine = cols[1, pl.ds(first_row, 512), :]
    rows0 = rows_ref[0:1, :].astype(F32)
    same = jnp.concatenate(
        [jnp.where(mine == rows0[:, 128 * m:128 * m + 128], 1.0, 0.0).astype(BF16) for m in range(8)], axis=1)
    out = dot(invs[1, :, pl.ds(first_row, 512)], same)
    noisy[...] = noise * (out[:128] + out[128:])
    left_own = left_side(desc, weights, log_amp)

    def side_by_side(s):
        return jnp.concatenate([slots[s, k] for k in range(CHIPS)], axis=1)

    def solved_copy(s, to):
        here = solved.at[s, core * DEPTH + z]
        return remote(here, here, s_solved.at[s], r_solved.at[s], to)

    def send_solved(s):
        for k in FAR_FIRST:
            for line in (r, sibling):
                solved_copy(s, (line, lax.rem(z + k, DEPTH))).start()
        solved_copy(s, (sibling, z)).start()

    def all_solved(s):
        here = solved.at[s, 0:2 * DEPTH - 1]
        return remote(here, here, s_solved.at[s], r_solved.at[s], (sibling, z))

    all_tiles(0).wait_recv()
    solved[0, core * DEPTH + z] = small_product(side_by_side(0), inv_slots[...])
    send_solved(0)

    for n in range(2):
        h = 1 - side if n == 0 else side
        some_points(8 - n, h).wait_recv()
        for s in range(2):
            block = jnp.concatenate([points_in[8 * h + k, 32 * s:32 * s + 32] for k in range(8)], axis=1)
            out = dot(stack3(block), onehot[s, pl.ds(pl.multiple_of(1024 * h, 1024), 1024), :])
            out = out[:32] + out[32:64] + out[64:]
            part_out[32 * s:32 * s + 32] = out if n == 0 else part_out[32 * s:32 * s + 32] + out
    part = remote(part_out, part_in, s_part, r_part, (sibling, z))
    part.start()
    all_tiles(1).wait_recv()
    out = dot(stack3(side_by_side(1)), onehot[1])
    panel1 = small_product(out[:8] + out[8:16] + out[16:], invs[1])
    part.wait_recv()
    block_points = part_out[...] + part_in[...]
    for s in range(2):
        right[s] = right_side(block_points[32 * s:32 * s + 32], weights)
    left[...] = left_side(block_points[32:64], weights, log_amp)

    total = noisy[...]
    for k in range(2):
        cut = pl.ds(pl.multiple_of(512 * core + 256 * k, 256), 256)
        high, low = parts2(jnp.exp(dot(left[:, cut], right[0], TN)))
        out = dot(invs[1, :, cut], high.astype(BF16))
        total = total + out[:128] + out[128:] + dot(invs[1, :128, cut], low.astype(BF16))
    ag[...] = stack2(total)

    def whole(s):
        return jnp.concatenate([solved[s, k] + solved[s, DEPTH + k] for k in range(DEPTH)], axis=1)

    def spread_copy(s, k, g):
        here = spread.at[s, core, chip]
        return remote(here, here, s_spread.at[s], r_spread.at[s, g], across(k))

    def group_spread(s, g):
        here = spread.at[s, 0, 0:len(GROUPS[g])]
        return remote(here, here, s_spread.at[s], r_spread.at[s, g], (sibling, z))

    def all_sent(s):
        here = spread.at[s, 0, 0:CHIPS - 1]
        return remote(here, here, s_spread.at[s], r_spread.at[s, 0], (sibling, z))

    def forward_copy(s, k):
        here = spread.at[s, core, shifted(k, -1)]
        return remote(here, here, s_fwd.at[s], r_fwd.at[s], (sibling, z))

    def all_forward(s):
        return remote(spread.at[s, 0], spread.at[s, 0], s_fwd.at[s], r_fwd.at[s], (sibling, z))

    def spread_out(s):
        spread[s, core, chip] = solved[s, pl.ds(4 * core, 4)] + solved[s, pl.ds(DEPTH + 4 * core, 4)]
        for g, group in enumerate(GROUPS):
            for k in group:
                spread_copy(s, k, g).start()
        forward_copy(s, (0, 0)).start()

    def pass_on(s):
        for g, group in enumerate(GROUPS):
            group_spread(s, g).wait_recv()
            for k in group:
                forward_copy(s, k).start()

    all_solved(0).wait_recv()
    solved[1, core * DEPTH + z] = panel1 - small_product(whole(0), ag[...])
    send_solved(1)
    spread_out(0)

    for s in range(2):
        high, low = parts2(jnp.exp(dot(left_own, right[s], TN)))
        kern[s, :256] = high.astype(BF16)
        kern[s, 256:512] = low.astype(BF16)
        own = iota((256, 1024), 0) + base == rows_ref[s:s + 1, :]
        kern[s, 512:] = jnp.where(own, 1.0, 0.0).astype(BF16)

    all_solved(1).wait_recv()
    spread_out(1)

    def change(s, h):
        update = jnp.concatenate([spread[s, h, :, k].reshape(128, 128) for k in range(4)], axis=1)
        out = dot(kern[s, :, pl.ds(pl.multiple_of(512 * h, 512), 512)], stack2(update), NT)
        smooth = out[:256, :128] + out[:256, 128:] + out[256:512, :128]
        return smooth, out[512:, :128] + out[512:, 128:]

    late[1].wait()
    smooth, moved = jnp.zeros((256, 128), F32), jnp.zeros((256, 128), F32)
    for s in range(2):
        pass_on(s)
        for h in (core, 1 - core):
            if h is not core:
                all_forward(s).wait_recv()
            more = change(s, h)
            smooth, moved = smooth + more[0], moved + more[1]
    sol_out[...] = sol_ref[...] + moved
    res_out[...] = res_ref[...] - smooth - noise * moved

    all_packs.wait_send()
    some_points(CHIPS - 1, 0).wait_send()
    part.wait_send()
    for s in range(2):
        all_lines(s).wait_send()
        all_tiles(s).wait_send()
        all_solved(s).wait_send()
        all_sent(s).wait_send()
        all_forward(s).wait_send()


def local(residual_in, solution_in, descriptors, length_weights, amplitude, noise, block_inverse, block_rows):
    vmem = pl.BlockSpec(memory_space=pltpu.VMEM)
    hbm = pl.BlockSpec(memory_space=pl.ANY)
    dma = pltpu.SemaphoreType.DMA
    shape = pltpu.VMEM(residual_in.shape, F32)
    return pl.pallas_call(
        kernel,
        out_shape=(shape, shape),
        in_specs=[hbm] * 8,
        out_specs=(vmem, vmem),
        scratch_shapes=[
            pltpu.VMEM((256, 128), F32),
            pltpu.VMEM((256, 128), F32),
            pltpu.VMEM((32, 256), F32),
            pltpu.VMEM((2, 128, 1024), F32),
            pltpu.VMEM((2, 1024), jnp.int32),
            pltpu.SMEM((32,), F32),
            pltpu.SMEM((1,), F32),
            pltpu.SMEM((1,), F32),
            pltpu.VMEM((2, 1024, 128), F32),
            pltpu.VMEM((2, 1024), jnp.int32),
            pltpu.VMEM((2, 2048, 1024), BF16),
            pltpu.VMEM((2, DEPTH, 16, 128), F32),
            pltpu.VMEM((DEPTH, 8, 128), F32),
            pltpu.VMEM((2, CHIPS, 8, 128), F32),
            pltpu.VMEM((2, CHIPS, 8, 128), F32),
            pltpu.VMEM((CHIPS, 64, 128), F32),
            pltpu.VMEM((64, 1024), F32),
            pltpu.VMEM((64, 1024), F32),
            pltpu.VMEM((2, 208, 1024), BF16),
            pltpu.VMEM((208, 1024), BF16),
            pltpu.VMEM((2, 256, 1024), BF16),
            pltpu.VMEM((256, 2048), BF16),
            pltpu.VMEM((128, 1024), F32),
            pltpu.VMEM((256, 1024), BF16),
            pltpu.VMEM((2, 2 * DEPTH, 8, 128), F32),
            pltpu.VMEM((2, 2, CHIPS, 4, 8, 128), F32),
            pltpu.VMEM((2, 768, 1024), BF16),
            dma((6,)), dma((2,)),
            dma((2,)), dma((2,)), dma, dma, dma((2,)), dma((2,)), dma, dma((2,)), dma, dma,
            dma((2,)), dma((2,)), dma((2,)), dma((2, len(GROUPS))), dma((2,)), dma((2,)),
        ],
        compiler_params=pltpu.CompilerParams(
            collective_id=0, has_side_effects=True, vmem_limit_bytes=VMEM_BYTES),
    )(residual_in, solution_in, descriptors, block_inverse, block_rows, length_weights, amplitude, noise)


def solution(mesh):
    placed = (
        P(("rows", "grp"), None),
        P(("rows", "grp"), None),
        P(None, ("rows", "grp")),
        P(),
        P(),
        P(),
        P(None, "grp", None),
        P(),
    )
    return jax.shard_map(
        local,
        mesh=mesh,
        in_specs=placed,
        out_specs=(P(("rows", "grp"), None), P(("rows", "grp"), None)),
        check_vma=False,
    )
```

time: 54.5 us -> 44.8 us (0.82)
  Pallas kernels: 50.2 us -> 41.4 us
  local copies, waits for them, and re-layouts: 2.26 us -> 1.31 us
    pallas_call x1, Pallas kernels: 50.2 us -> 41.4 us  [local(): pl.pallas_call(kernel, out_shape=(shape, shape), in_specs=[hbm] * 8, out_...]
    unnamed x4 -> x2, local copies, waits for them, and re-layouts: 2.26 us -> 1.31 us
where the time goes in v2:
time: 44.8 us; the launch traced here: 44.7 us
  Pallas kernels  41.4 us (92%)
  between operations  1.93 us (4%)
  local copies, waits for them, and re-layouts  1.31 us (3%)
    pallas_call x1, Pallas kernels, local(): pl.pallas_call(kernel, out_shape=(shape, shape), in_specs=[hbm] * 8, out_...  41.4 us
    unnamed x2, local copies, waits for them, and re-layouts  1.31 us

profile of v2, /device:TPU:1, one launch (start us, length us, event | category | flops | bytes accessed | tf_op | source)
XLA Modules:
  0.0 44.7 jit_solution(5594901764751736859)
XLA Ops:
  1.9 41.4 %shard_map.95 = (f32[256,128]{1,0:T(8,128)S(1)}, f32[256,128]{1,0:T(8,128)S(1)}) custom-call(f32[256,128]{1,0:T(8,128)} %res_hbm.1, f32[256,128]{1,0:T(8,128)} %sol_hbm.1, f32[32,256]{1,0:T(8,128)} %desc_hbm.1, f32[2,128,1024]{2,1,0:T(8,128)} %inv_hbm.1, s32[2,1024]{1,0:T(2,128)} %rows_hbm.1, f32[32]{0:T(128)} %w_hbm.1, f32[1]{0:T(128)S(6)} %copy.14.amp_hbm, ...), custom_call_target="tpu_custom_call" | custom-call | tf_op jit(solution)/shard_map/pallas_call | solution.py:406
  43.4 0.7 %copy.12 = f32[256,128]{1,0:T(8,128)} copy(f32[256,128]{1,0:T(8,128)S(1)} %get-tuple-element.2) | data formatting | bytes 262144
  44.0 0.7 %copy.13 = f32[256,128]{1,0:T(8,128)} copy(f32[256,128]{1,0:T(8,128)S(1)} %get-tuple-element.3) | data formatting | bytes 262144

commit v3 on v2

--- a/solution.py
+++ b/solution.py
@@ -10,10 +10,10 @@
 BF16 = jnp.bfloat16
 LINES, DEPTH, CHIPS = 32, 8, 16
 FAR_FIRST = (4, 3, 5, 2, 6, 1, 7)
+ORDER = (0, 1, 7, 2, 3, 5, 4, 6)
 OFFSETS = sorted(
     ((a, b) for a in range(4) for b in range(4) if a or b),
     key=lambda o: -(min(o[0], 4 - o[0]) + min(o[1], 4 - o[1])))
-GROUPS = (OFFSETS[:5], OFFSETS[5:10], OFFSETS[10:])
 VMEM_BYTES = 56 * 1024 * 1024
 NT = (((1,), (1,)), ((), ()))
 TN = (((0,), (0,)), ((), ()))
@@ -87,6 +87,7 @@
     chip, core = lax.div(r, 2), lax.rem(r, 2)
     sibling = r + 1 - 2 * core
     base = (r * DEPTH + z) * 256
+    panels = [pl.multiple_of(128 * lax.rem(z + q, DEPTH), 128) for q in ORDER]
 
     loads = [
         pltpu.make_async_copy(a, b, load_sem.at[k])
@@ -111,8 +112,7 @@
 
     lax.fori_loop(1, DEPTH, greet_depth, 0)
     lax.fori_loop(1, LINES, greet_plane, 0)
-    for copy in loads[:2]:
-        copy.wait()
+    loads[0].wait()
     before = (iota((256, 256), 0) < iota((256, 256), 1)).astype(F32).astype(BF16)
 
     def pick(s):
@@ -127,13 +127,16 @@
         member = jnp.concatenate(member, axis=1)
         rank = dot(jnp.broadcast_to(member, (16, 256)).astype(BF16), before)
         slot = iota((16, 256), 0).astype(F32)
-        mine = jnp.where((rank == slot) & (member > 0.5), 1.0, 0.0).astype(BF16)
-        out = dot(mine, split_res)
+        return jnp.where((rank == slot) & (member > 0.5), 1.0, 0.0).astype(BF16)
+
+    def fill_line(s):
+        out = dot(picks[s], split_res)
         lines[s, z] = out[:, :128] + out[:, 128:256] + out[:, 256:]
-        return mine
-
+
+    picks = [pick(0)]
+    loads[1].wait()
     split_res = jnp.concatenate(parts3(res_ref[...]), axis=1).astype(BF16)
-    picks = [pick(0)]
+    fill_line(0)
     pl.semaphore_wait(barrier, 2 * (DEPTH - 1) + LINES - 1)
 
     def remote(src, dst, send, recv, to):
@@ -157,6 +160,7 @@
     for k in FAR_FIRST:
         line_copy(0, k).start()
     picks.append(pick(1))
+    fill_line(1)
     for copy in loads[2:]:
         copy.wait()
     noise = noise_ref[0]
@@ -182,6 +186,9 @@
     for s in range(2):
         invs[s] = stack2(inv_ref[s])
 
+    def rows_in_order(s):
+        return jnp.concatenate([rows_ref[s:s + 1, pl.ds(p, 128)] for p in panels], axis=1)
+
     def slot_ids(s):
         rows = rows_ref[s:s + 1, :]
         owner = lax.shift_right_logical(rows, 8)
@@ -264,7 +271,7 @@
     fill_onehot(1)
     first_row = pl.multiple_of(512 * core, 512)
     mine = cols[1, pl.ds(first_row, 512), :]
-    rows0 = rows_ref[0:1, :].astype(F32)
+    rows0 = rows_in_order(0).astype(F32)
     same = jnp.concatenate(
         [jnp.where(mine == rows0[:, 128 * m:128 * m + 128], 1.0, 0.0).astype(BF16) for m in range(8)], axis=1)
     out = dot(invs[1, :, pl.ds(first_row, 512)], same)
@@ -274,23 +281,34 @@
     def side_by_side(s):
         return jnp.concatenate([slots[s, k] for k in range(CHIPS)], axis=1)
 
-    def solved_copy(s, to):
-        here = solved.at[s, core * DEPTH + z]
-        return remote(here, here, s_solved.at[s], r_solved.at[s], to)
+    def solved_copy(s, k, line):
+        slot = ORDER.index((DEPTH - k) % DEPTH)
+        return remote(
+            solved.at[s, core * DEPTH], solved.at[s, core * DEPTH + slot],
+            s_solved.at[s], r_solved.at[s, slot // 4], (line, lax.rem(z + k, DEPTH)))
 
     def send_solved(s):
         for k in FAR_FIRST:
             for line in (r, sibling):
-                solved_copy(s, (line, lax.rem(z + k, DEPTH))).start()
-        solved_copy(s, (sibling, z)).start()
-
-    def all_solved(s):
-        here = solved.at[s, 0:2 * DEPTH - 1]
-        return remote(here, here, s_solved.at[s], r_solved.at[s], (sibling, z))
+                solved_copy(s, k, line).start()
+        solved_copy(s, 0, sibling).start()
+
+    def some_solved(s, n, far):
+        here = solved.at[s, 0:n]
+        return remote(here, here, s_solved.at[s], r_solved.at[s, far], (sibling, z))
+
+    def near_solved(s):
+        some_solved(s, 7, 0).wait_recv()
+
+    def far_solved(s):
+        some_solved(s, 8, 1).wait_recv()
 
     all_tiles(0).wait_recv()
-    solved[0, core * DEPTH + z] = small_product(side_by_side(0), inv_slots[...])
+    solved[0, core * DEPTH] = small_product(side_by_side(0), inv_slots[...])
     send_solved(0)
+
+    def part_copy(s):
+        return remote(part_out.at[s], part_in.at[s], s_part.at[s], r_part.at[s], (sibling, z))
 
     for n in range(2):
         h = 1 - side if n == 0 else side
@@ -299,17 +317,18 @@
             block = jnp.concatenate([points_in[8 * h + k, 32 * s:32 * s + 32] for k in range(8)], axis=1)
             out = dot(stack3(block), onehot[s, pl.ds(pl.multiple_of(1024 * h, 1024), 1024), :])
             out = out[:32] + out[32:64] + out[64:]
-            part_out[32 * s:32 * s + 32] = out if n == 0 else part_out[32 * s:32 * s + 32] + out
-    part = remote(part_out, part_in, s_part, r_part, (sibling, z))
-    part.start()
+            part_out[s] = out if n == 0 else part_out[s] + out
+            if n == 1:
+                part_copy(s).start()
     all_tiles(1).wait_recv()
     out = dot(stack3(side_by_side(1)), onehot[1])
     panel1 = small_product(out[:8] + out[8:16] + out[16:], invs[1])
-    part.wait_recv()
-    block_points = part_out[...] + part_in[...]
-    for s in range(2):
-        right[s] = right_side(block_points[32 * s:32 * s + 32], weights)
-    left[...] = left_side(block_points[32:64], weights, log_amp)
+    for s in range(2):
+        part_copy(s).wait_recv()
+        right[s] = right_side(
+            jnp.concatenate([part_out[s, :, pl.ds(p, 128)] + part_in[s, :, pl.ds(p, 128)] for p in panels], axis=1),
+            weights)
+    left[...] = left_side(part_out[1] + part_in[1], weights, log_amp)
 
     total = noisy[...]
     for k in range(2):
@@ -322,20 +341,18 @@
     def whole(s):
         return jnp.concatenate([solved[s, k] + solved[s, DEPTH + k] for k in range(DEPTH)], axis=1)
 
-    def spread_copy(s, k, g):
+    row_of_chips = lax.div(chip, 4)
+
+    def spread_copy(s, offset):
         here = spread.at[s, core, chip]
-        return remote(here, here, s_spread.at[s], r_spread.at[s, g], across(k))
-
-    def group_spread(s, g):
-        here = spread.at[s, 0, 0:len(GROUPS[g])]
-        return remote(here, here, s_spread.at[s], r_spread.at[s, g], (sibling, z))
-
-    def all_sent(s):
-        here = spread.at[s, 0, 0:CHIPS - 1]
-        return remote(here, here, s_spread.at[s], r_spread.at[s, 0], (sibling, z))
-
-    def forward_copy(s, k):
-        here = spread.at[s, core, shifted(k, -1)]
+        return remote(here, here, s_spread.at[s], r_spread.at[s, row_of_chips], across(offset))
+
+    def some_spread(s, n, source):
+        here = spread.at[s, 0, 0:n]
+        return remote(here, here, s_spread.at[s], r_spread.at[s, source], (sibling, z))
+
+    def forward_copy(s, source):
+        here = spread.at[s, core, pl.ds(4 * source, 4)]
         return remote(here, here, s_fwd.at[s], r_fwd.at[s], (sibling, z))
 
     def all_forward(s):
@@ -343,19 +360,18 @@
 
     def spread_out(s):
         spread[s, core, chip] = solved[s, pl.ds(4 * core, 4)] + solved[s, pl.ds(DEPTH + 4 * core, 4)]
-        for g, group in enumerate(GROUPS):
-            for k in group:
-                spread_copy(s, k, g).start()
-        forward_copy(s, (0, 0)).start()
+        for offset in OFFSETS:
+            spread_copy(s, offset).start()
 
     def pass_on(s):
-        for g, group in enumerate(GROUPS):
-            group_spread(s, g).wait_recv()
-            for k in group:
-                forward_copy(s, k).start()
-
-    all_solved(0).wait_recv()
-    solved[1, core * DEPTH + z] = panel1 - small_product(whole(0), ag[...])
+        for k in (0, 1, 3, 2):
+            source = lax.rem(row_of_chips + k, 4)
+            some_spread(s, 4 if k else 3, source).wait_recv()
+            forward_copy(s, source).start()
+
+    near_solved(0)
+    far_solved(0)
+    solved[1, core * DEPTH] = panel1 - small_product(whole(0), ag[...])
     send_solved(1)
     spread_out(0)
 
@@ -363,10 +379,17 @@
         high, low = parts2(jnp.exp(dot(left_own, right[s], TN)))
         kern[s, :256] = high.astype(BF16)
         kern[s, 256:512] = low.astype(BF16)
-        own = iota((256, 1024), 0) + base == rows_ref[s:s + 1, :]
+        own = iota((256, 1024), 0) + base == rows_in_order(s)
         kern[s, 512:] = jnp.where(own, 1.0, 0.0).astype(BF16)
 
-    all_solved(1).wait_recv()
+    @pl.when(core == 0)
+    def _():
+        near_solved(1)
+
+    @pl.when(core == 1)
+    def _():
+        far_solved(1)
+
     spread_out(1)
 
     def change(s, h):
@@ -387,14 +410,23 @@
     sol_out[...] = sol_ref[...] + moved
     res_out[...] = res_ref[...] - smooth - noise * moved
 
+    @pl.when(core == 0)
+    def _():
+        far_solved(1)
+
+    @pl.when(core == 1)
+    def _():
+        near_solved(1)
+
     all_packs.wait_send()
     some_points(CHIPS - 1, 0).wait_send()
-    part.wait_send()
+    for s in range(2):
+        part_copy(s).wait_send()
     for s in range(2):
         all_lines(s).wait_send()
         all_tiles(s).wait_send()
-        all_solved(s).wait_send()
-        all_sent(s).wait_send()
+        some_solved(s, 15, 0).wait_send()
+        some_spread(s, CHIPS - 1, 0).wait_send()
         all_forward(s).wait_send()
 
 
@@ -425,8 +457,8 @@
             pltpu.VMEM((2, CHIPS, 8, 128), F32),
             pltpu.VMEM((2, CHIPS, 8, 128), F32),
             pltpu.VMEM((CHIPS, 64, 128), F32),
-            pltpu.VMEM((64, 1024), F32),
-            pltpu.VMEM((64, 1024), F32),
+            pltpu.VMEM((2, 32, 1024), F32),
+            pltpu.VMEM((2, 32, 1024), F32),
             pltpu.VMEM((2, 208, 1024), BF16),
             pltpu.VMEM((208, 1024), BF16),
             pltpu.VMEM((2, 256, 1024), BF16),
@@ -437,8 +469,8 @@
             pltpu.VMEM((2, 2, CHIPS, 4, 8, 128), F32),
             pltpu.VMEM((2, 768, 1024), BF16),
             dma((6,)), dma((2,)),
-            dma((2,)), dma((2,)), dma, dma, dma((2,)), dma((2,)), dma, dma((2,)), dma, dma,
-            dma((2,)), dma((2,)), dma((2,)), dma((2, len(GROUPS))), dma((2,)), dma((2,)),
+            dma((2,)), dma((2,)), dma, dma, dma((2,)), dma((2,)), dma, dma((2,)), dma((2,)), dma((2,)),
+            dma((2,)), dma((2, 2)), dma((2,)), dma((2, 4)), dma((2,)), dma((2,)),
         ],
         compiler_params=pltpu.CompilerParams(
             collective_id=0, has_side_effects=True, vmem_limit_bytes=VMEM_BYTES),

time: 44.8 us -> 44.9 us (level)
  no operation moved by 1% of the time
where the time goes in v3:
time: 44.9 us; the launch traced here: 44.8 us
  Pallas kernels  41.5 us (92%)
  between operations  1.93 us (4%)
  local copies, waits for them, and re-layouts  1.31 us (3%)
    pallas_call x1, Pallas kernels, local(): pl.pallas_call(kernel, out_shape=(shape, shape), in_specs=[hbm] * 8, out_...  41.5 us
    unnamed x2, local copies, waits for them, and re-layouts  1.31 us

profile of v3, /device:TPU:1, one launch (start us, length us, event | category | flops | bytes accessed | tf_op | source)
XLA Modules:
  0.0 44.8 jit_solution(6374359122965210990)
XLA Ops:
  1.9 41.5 %shard_map.95 = (f32[256,128]{1,0:T(8,128)S(1)}, f32[256,128]{1,0:T(8,128)S(1)}) custom-call(f32[256,128]{1,0:T(8,128)} %res_hbm.1, f32[256,128]{1,0:T(8,128)} %sol_hbm.1, f32[32,256]{1,0:T(8,128)} %desc_hbm.1, f32[2,128,1024]{2,1,0:T(8,128)} %inv_hbm.1, s32[2,1024]{1,0:T(2,128)} %rows_hbm.1, f32[32]{0:T(128)} %w_hbm.1, f32[1]{0:T(128)S(6)} %copy.14.amp_hbm, ...), custom_call_target="tpu_custom_call" | custom-call | tf_op jit(solution)/shard_map/pallas_call | solution.py:438
  43.5 0.7 %copy.12 = f32[256,128]{1,0:T(8,128)} copy(f32[256,128]{1,0:T(8,128)S(1)} %get-tuple-element.2) | data formatting | bytes 262144
  44.1 0.7 %copy.13 = f32[256,128]{1,0:T(8,128)} copy(f32[256,128]{1,0:T(8,128)S(1)} %get-tuple-element.3) | data formatting | bytes 262144

commit v4 on v2

--- a/solution.py
+++ b/solution.py
@@ -10,6 +10,7 @@
 BF16 = jnp.bfloat16
 LINES, DEPTH, CHIPS = 32, 8, 16
 FAR_FIRST = (4, 3, 5, 2, 6, 1, 7)
+ORDER = (0, 1, 7, 2, 3, 5, 4, 6)
 OFFSETS = sorted(
     ((a, b) for a in range(4) for b in range(4) if a or b),
     key=lambda o: -(min(o[0], 4 - o[0]) + min(o[1], 4 - o[1])))
@@ -87,6 +88,7 @@
     chip, core = lax.div(r, 2), lax.rem(r, 2)
     sibling = r + 1 - 2 * core
     base = (r * DEPTH + z) * 256
+    panels = [pl.multiple_of(128 * lax.rem(z + q, DEPTH), 128) for q in ORDER]
 
     loads = [
         pltpu.make_async_copy(a, b, load_sem.at[k])
@@ -182,6 +184,9 @@
     for s in range(2):
         invs[s] = stack2(inv_ref[s])
 
+    def rows_in_order(s):
+        return jnp.concatenate([rows_ref[s:s + 1, pl.ds(p, 128)] for p in panels], axis=1)
+
     def slot_ids(s):
         rows = rows_ref[s:s + 1, :]
         owner = lax.shift_right_logical(rows, 8)
@@ -264,7 +269,7 @@
     fill_onehot(1)
     first_row = pl.multiple_of(512 * core, 512)
     mine = cols[1, pl.ds(first_row, 512), :]
-    rows0 = rows_ref[0:1, :].astype(F32)
+    rows0 = rows_in_order(0).astype(F32)
     same = jnp.concatenate(
         [jnp.where(mine == rows0[:, 128 * m:128 * m + 128], 1.0, 0.0).astype(BF16) for m in range(8)], axis=1)
     out = dot(invs[1, :, pl.ds(first_row, 512)], same)
@@ -274,22 +279,30 @@
     def side_by_side(s):
         return jnp.concatenate([slots[s, k] for k in range(CHIPS)], axis=1)
 
-    def solved_copy(s, to):
-        here = solved.at[s, core * DEPTH + z]
-        return remote(here, here, s_solved.at[s], r_solved.at[s], to)
+    def solved_copy(s, k, line):
+        slot = ORDER.index((DEPTH - k) % DEPTH)
+        return remote(
+            solved.at[s, core * DEPTH], solved.at[s, core * DEPTH + slot],
+            s_solved.at[s], r_solved.at[s, slot // 4], (line, lax.rem(z + k, DEPTH)))
 
     def send_solved(s):
         for k in FAR_FIRST:
             for line in (r, sibling):
-                solved_copy(s, (line, lax.rem(z + k, DEPTH))).start()
-        solved_copy(s, (sibling, z)).start()
-
-    def all_solved(s):
-        here = solved.at[s, 0:2 * DEPTH - 1]
-        return remote(here, here, s_solved.at[s], r_solved.at[s], (sibling, z))
+                solved_copy(s, k, line).start()
+        solved_copy(s, 0, sibling).start()
+
+    def some_solved(s, n, far):
+        here = solved.at[s, 0:n]
+        return remote(here, here, s_solved.at[s], r_solved.at[s, far], (sibling, z))
+
+    def near_solved(s):
+        some_solved(s, 7, 0).wait_recv()
+
+    def far_solved(s):
+        some_solved(s, 8, 1).wait_recv()
 
     all_tiles(0).wait_recv()
-    solved[0, core * DEPTH + z] = small_product(side_by_side(0), inv_slots[...])
+    solved[0, core * DEPTH] = small_product(side_by_side(0), inv_slots[...])
     send_solved(0)
 
     for n in range(2):
@@ -306,10 +319,12 @@
     out = dot(stack3(side_by_side(1)), onehot[1])
     panel1 = small_product(out[:8] + out[8:16] + out[16:], invs[1])
     part.wait_recv()
-    block_points = part_out[...] + part_in[...]
     for s in range(2):
-        right[s] = right_side(block_points[32 * s:32 * s + 32], weights)
-    left[...] = left_side(block_points[32:64], weights, log_amp)
+        right[s] = right_side(jnp.concatenate(
+            [part_out[32 * s:32 * s + 32, pl.ds(p, 128)] + part_in[32 * s:32 * s + 32, pl.ds(p, 128)] for p in panels],
+            axis=1), weights)
+        if s == 0:
+            left[...] = left_side(part_out[32:] + part_in[32:], weights, log_amp)
 
     total = noisy[...]
     for k in range(2):
@@ -354,8 +369,9 @@
             for k in group:
                 forward_copy(s, k).start()
 
-    all_solved(0).wait_recv()
-    solved[1, core * DEPTH + z] = panel1 - small_product(whole(0), ag[...])
+    near_solved(0)
+    far_solved(0)
+    solved[1, core * DEPTH] = panel1 - small_product(whole(0), ag[...])
     send_solved(1)
     spread_out(0)
 
@@ -363,10 +379,17 @@
         high, low = parts2(jnp.exp(dot(left_own, right[s], TN)))
         kern[s, :256] = high.astype(BF16)
         kern[s, 256:512] = low.astype(BF16)
-        own = iota((256, 1024), 0) + base == rows_ref[s:s + 1, :]
+        own = iota((256, 1024), 0) + base == rows_in_order(s)
         kern[s, 512:] = jnp.where(own, 1.0, 0.0).astype(BF16)
 
-    all_solved(1).wait_recv()
+    @pl.when(core == 0)
+    def _():
+        near_solved(1)
+
+    @pl.when(core == 1)
+    def _():
+        far_solved(1)
+
     spread_out(1)
 
     def change(s, h):
@@ -387,13 +410,21 @@
     sol_out[...] = sol_ref[...] + moved
     res_out[...] = res_ref[...] - smooth - noise * moved
 
+    @pl.when(core == 0)
+    def _():
+        far_solved(1)
+
+    @pl.when(core == 1)
+    def _():
+        near_solved(1)
+
     all_packs.wait_send()
     some_points(CHIPS - 1, 0).wait_send()
     part.wait_send()
     for s in range(2):
         all_lines(s).wait_send()
         all_tiles(s).wait_send()
-        all_solved(s).wait_send()
+        some_solved(s, 15, 0).wait_send()
         all_sent(s).wait_send()
         all_forward(s).wait_send()
 
@@ -438,7 +469,7 @@
             pltpu.VMEM((2, 768, 1024), BF16),
             dma((6,)), dma((2,)),
             dma((2,)), dma((2,)), dma, dma, dma((2,)), dma((2,)), dma, dma((2,)), dma, dma,
-            dma((2,)), dma((2,)), dma((2,)), dma((2, len(GROUPS))), dma((2,)), dma((2,)),
+            dma((2,)), dma((2, 2)), dma((2,)), dma((2, len(GROUPS))), dma((2,)), dma((2,)),
         ],
         compiler_params=pltpu.CompilerParams(
             collective_id=0, has_side_effects=True, vmem_limit_bytes=VMEM_BYTES),

time: 44.8 us -> 44.7 us (level)
  no operation moved by 1% of the time
where the time goes in v4:
time: 44.7 us; the launch traced here: 44.6 us
  Pallas kernels  41.3 us (92%)
  between operations  1.93 us (4%)
  local copies, waits for them, and re-layouts  1.31 us (3%)
    pallas_call x1, Pallas kernels, local(): pl.pallas_call(kernel, out_shape=(shape, shape), in_specs=[hbm] * 8, out_...  41.3 us
    unnamed x2, local copies, waits for them, and re-layouts  1.31 us

profile of v4, /device:TPU:1, one launch (start us, length us, event | category | flops | bytes accessed | tf_op | source)
XLA Modules:
  0.0 44.6 jit_solution(4890318238741545067)
XLA Ops:
  1.9 41.3 %shard_map.95 = (f32[256,128]{1,0:T(8,128)S(1)}, f32[256,128]{1,0:T(8,128)S(1)}) custom-call(f32[256,128]{1,0:T(8,128)} %res_hbm.1, f32[256,128]{1,0:T(8,128)} %sol_hbm.1, f32[32,256]{1,0:T(8,128)} %desc_hbm.1, f32[2,128,1024]{2,1,0:T(8,128)} %inv_hbm.1, s32[2,1024]{1,0:T(2,128)} %rows_hbm.1, f32[32]{0:T(128)} %w_hbm.1, f32[1]{0:T(128)S(6)} %copy.14.amp_hbm, ...), custom_call_target="tpu_custom_call" | custom-call | tf_op jit(solution)/shard_map/pallas_call | solution.py:437
  43.3 0.7 %copy.12 = f32[256,128]{1,0:T(8,128)} copy(f32[256,128]{1,0:T(8,128)S(1)} %get-tuple-element.2) | data formatting | bytes 262144
  43.9 0.7 %copy.13 = f32[256,128]{1,0:T(8,128)} copy(f32[256,128]{1,0:T(8,128)S(1)} %get-tuple-element.3) | data formatting | bytes 262144
